TPU v7x, 32 devices: a whole 2x2x4 slice. The times are simulated.
32 devices in a mesh: group: 2 (over y), seq: 4 (over z), tensor: 4 (over x, core).
Axes of the slice: x: 2, y: 2, z: 4, core: 2. Of those that a mesh axis runs over, the one named last changes fastest.
Arguments:
- spans: bfloat16 [1024, 3072], P(('group', 'seq')), parts along dimension 0, may hold values from -6 to 6
- w_in: bfloat16 [3072, 1024], P(None, 'tensor'), may hold values from -0.109375 to 0.109375
- band_weights: bfloat16 [4096, 128], P(('group', 'seq')), parts along dimension 0
- offsets: int32 [32], P(('group', 'seq')), parts along dimension 0, may hold values from 0 to 384, as said below
- w_up: bfloat16 [1024, 4096], P(None, 'tensor'), may hold values from -0.1875 to 0.1875
- d_up: bfloat16 [4096, 4096], P(('group', 'seq'), 'tensor'), parts along dimension 0, may hold values from -3 to 3
Outputs:
- up_proj: bfloat16 [4096, 4096], P(('group', 'seq'), 'tensor'), parts along dimension 0
- d_spans: bfloat16 [1024, 3072], P(('group', 'seq'), 'tensor'), parts along dimension 0
There are 2 independent parts, one for each index of `group`. A program takes and returns all parts, laid end to end along the dimension named above; an argument that names none is the same for every part. Nothing has to cross between parts.
Inputs may be any that keep to these rules, and one draw needn't show every extreme that they name: offsets[b] differs from b * 384 // 15 by at most 128, and both differences -128 and +128 occur in every draw; offsets[0] = 0 and offsets[15] = 384. Hence the bands of the bytes of seq index i lie within the span rows of seq indices i - 3 to i + 3.
All inputs are finite; a program needn't handle non-finite values.
Results may differ from a plain program's by a relative error of at most 0.0058.
Values may be sent and summed in bfloat16 or wider, within the bound.
No kernel may reach another device: no remote copies, remote signals or barrier semaphores. Data moves between devices by JAX's collectives and lax.ppermute only.
A program may use at most 64 MiB of HBM per device.

v0:
```python
import jax
import jax.numpy as jnp
from jax import lax
from jax.sharding import PartitionSpec as P


def band_matrix(band_weights, offsets, anchor, length):
    blocks = offsets.shape[0]
    breadth = band_weights.shape[1]
    band_cube = band_weights.reshape(blocks, -1, breadth)
    relative = anchor + jnp.arange(length, dtype=jnp.int32)[None, :] - offsets[:, None]
    picker = (relative[:, None, :] == jnp.arange(breadth, dtype=jnp.int32)[None, :, None]).astype(
        jnp.bfloat16
    )
    spread = jnp.einsum("bij,bjr->bir", band_cube, picker, preferred_element_type=jnp.float32)
    return spread.astype(jnp.bfloat16).reshape(-1, length)


def touches(offsets, breadth, anchor, length):
    return jnp.any((offsets < anchor + length) & (offsets + breadth > anchor))


def body(spans, w_in, band_weights, offsets, w_up, d_up):
    breadth = band_weights.shape[1]
    reduced = jnp.dot(spans, w_in, preferred_element_type=jnp.float32).astype(jnp.bfloat16)
    feature_count = reduced.shape[1]
    span_rows = reduced.shape[0]
    initial = jnp.zeros((band_weights.shape[0], feature_count), jnp.float32)
    shard_rows = lax.all_gather(reduced, "seq", axis=0, tiled=True)
    anchor = jnp.int32(0)
    length = shard_rows.shape[0]

    def accumulate(current):
        spread = band_matrix(band_weights, offsets, anchor, length)
        return jnp.dot(spread, shard_rows, preferred_element_type=jnp.float32)

    def unchanged(current):
        return current

    upsampled = lax.cond(
        touches(offsets, breadth, anchor, length), accumulate, unchanged, initial
    ).astype(jnp.bfloat16)
    gathered = lax.all_gather(upsampled, "tensor", axis=1, tiled=True)
    up_proj = jnp.dot(gathered, w_up, preferred_element_type=jnp.float32).astype(jnp.bfloat16)
    grad_cols = lax.psum_scatter(
        lax.dot_general(w_up, d_up, (((1,), (1,)), ((), ())), preferred_element_type=jnp.float32),
        "tensor",
        scatter_dimension=0,
        tiled=True,
    ).astype(jnp.bfloat16)

    def compute(operand):
        spread = band_matrix(band_weights, offsets, 0, span_rows * lax.axis_size("seq"))
        return lax.dot_general(
            spread, grad_cols, (((0,), (1,)), ((), ())), preferred_element_type=jnp.float32
        )

    def nothing(operand):
        return jnp.zeros((span_rows * lax.axis_size("seq"), feature_count), jnp.float32)

    every_row = lax.psum(
        lax.cond(
            touches(offsets, breadth, 0, span_rows * lax.axis_size("seq")), compute, nothing, 0
        ),
        "seq",
    )
    d_reduced = lax.dynamic_slice_in_dim(every_row, lax.axis_index("seq") * span_rows, span_rows, 0)
    d_reduced = d_reduced.astype(jnp.bfloat16)
    feature_parts = lax.dot_general(
        d_reduced, w_in, (((1,), (1,)), ((), ())), preferred_element_type=jnp.float32
    )
    d_spans = lax.psum_scatter(feature_parts, "tensor", scatter_dimension=1, tiled=True).astype(
        jnp.bfloat16
    )
    return (up_proj, d_spans)


def solution(mesh):
    placed = (
        P(("group", "seq"), None),
        P(None, "tensor"),
        P(("group", "seq"), None),
        P(("group", "seq")),
        P(None, "tensor"),
        P(("group", "seq"), "tensor"),
    )
    return jax.shard_map(
        body,
        mesh=mesh,
        in_specs=placed,
        out_specs=(P(("group", "seq"), "tensor"), P(("group", "seq"), "tensor")),
        check_vma=False,
    )
```

profile of v0, /device:TPU:0, one launch (start us, length us, event | category | flops | bytes accessed | tf_op | source)
XLA Modules:
  0.0 116.6 jit_solution(14578127177563211295)
XLA Ops:
  7.2 1.5 %copy-done = bf16[1024,1024]{1,0:T(8,128)(2,1)S(1)} copy-done((bf16[1024,1024]{1,0:T(8,128)(2,1)S(1)}, bf16[1024,1024]{1,0:T(8,128)(2,1)}, u32[]{:S(2)}) %copy-start) | copy-done | bytes 2097176
  8.8 3.9 %fusion.6 = f32[1024,512]{1,0:T(8,128)} fusion(bf16[1024,1024]{1,0:T(8,128)(2,1)S(1)} %copy-done, bf16[512,1024]{1,0:T(8,128)(2,1)} %param.15), kind=kOutput, calls=%fused_computation.16 | convolution fusion | flops 1073741824 | bytes 5242880 | tf_op jit(solution)/shard_map/dot_general | solution.py:46
  12.7 0.0 all-gather.2.cloned.1.call-start
  12.7 0.6 copy-done.4
  13.3 0.6 and_reduce_fusion
  14.6 1.8 %convolution_convert_fusion.3 = bf16[128,256]{1,0:T(8,128)(2,1)S(1)} fusion(bf16[128,3072]{1,0:T(8,128)(2,1)S(1)} %copy-done.2, bf16[3072,256]{1,0:T(8,128)(2,1)} %param.11), kind=kOutput, calls=%fused_computation.9 | convolution fusion | flops 201359360 | bytes 2424832 | tf_op jit(solution)/shard_map/dot_general | solution.py:25
  16.4 15.6 %all_gather.6 = bf16[512,256]{1,0:T(8,128)(2,1)S(1)} all-gather(bf16[128,256]{1,0:T(8,128)(2,1)S(1)} %convolution_convert_fusion.3), channel_id=1, replica_groups=mesh['group'=2,'seq'=4,'tensor'=4] {'seq'}, dimensions={0}, use_global_device_ids=true | all-gather | bytes 327680 | tf_op jit(solution)/shard_map/all_gather | solution.py:29
  32.0 0.7 conditional.2
  32.0 0.1 iota_subtract_fusion
  32.1 0.3 convolution_convert_fusion
  32.4 0.3 fusion.4
  32.7 0.7 copy-done.1
  33.5 0.0 reduce-scatter.5.cloned.1.call-start
  33.5 13.4 %reduce-scatter.3.cloned.1.call-done = f32[256,512]{1,0:T(8,128)} async-done(((f32[1024,512]{1,0:T(8,128)}), f32[256,512]{1,0:T(8,128)}) %reduce-scatter.3.cloned.1.call-update) | async-done | bytes 524304 | tf_op jit(solution)/shard_map/reduce_scatter | solution.py:45
  46.9 1.1 convert_element_type.40
  48.0 0.8 conditional.3
  48.0 0.1 iota_subtract_fusion.1
  48.1 0.3 convolution_convert_fusion.1
  48.5 0.3 fusion.5
  48.8 30.5 %all-reduce.1 = bf16[512,256]{1,0:T(8,128)(2,1)S(1)} all-reduce(f32[512,256]{1,0:T(8,128)S(1)} %get-tuple-element.27), channel_id=1, replica_groups=mesh['group'=2,'seq'=4,'tensor'=4] {'seq'}, use_global_device_ids=true, to_apply=%region_6.0 | all-reduce | flops 131072 | bytes 786432 | tf_op jit(solution)/shard_map/psum | solution.py:61
  79.3 3.2 %fusion.2 = f32[128,3072]{1,0:T(8,128)} fusion(bf16[3072,256]{1,0:T(8,128)(2,1)} %param.11, bf16[512,256]{1,0:T(8,128)(2,1)S(1)} %all-reduce.1, s32[]{:T(128)S(6)} %select_n.3), kind=kOutput, calls=%fused_computation.11 | convolution fusion | flops 201326592 | bytes 3211268 | tf_op jit(solution)/shard_map/dot_general | solution.py:69
  82.5 3.4 %convolution_convert_fusion.2 = bf16[512,1024]{1,0:T(8,128)(2,1)} fusion(bf16[512,1024]{1,0:T(8,128)(2,1)} %all-gather.2.cloned.1.call-done, bf16[1024,1024]{1,0:T(8,128)(2,1)S(1)} %copy-done), kind=kOutput, calls=%fused_computation.8 | convolution fusion | flops 1074266112 | bytes 4194304 | tf_op jit(solution)/shard_map/dot_general | solution.py:44
  86.0 22.4 %reduce-scatter.5.cloned.1.call-done = f32[128,768]{1,0:T(8,128)} async-done(((f32[128,3072]{1,0:T(8,128)}), f32[128,768]{1,0:T(8,128)}) %reduce-scatter.5.cloned.1.call-update) | async-done | bytes 393232 | tf_op jit(solution)/shard_map/reduce_scatter | solution.py:72
  108.4 1.7 %convert_element_type.42 = bf16[128,768]{1,0:T(8,128)(2,1)} convert(f32[128,768]{1,0:T(8,128)} %reduce-scatter.5.cloned.1.call-done) | non-fusion elementwise | flops 98304 | bytes 589824 | tf_op jit(solution)/shard_map/convert_element_type | solution.py:72
  (12 shorter events, 0.1 us)
Async XLA Ops:
  7.2 1.6 %copy-start = (bf16[1024,1024]{1,0:T(8,128)(2,1)S(1)}, bf16[1024,1024]{1,0:T(8,128)(2,1)}, u32[]{:S(2)}) copy-start(bf16[1024,1024]{1,0:T(8,128)(2,1)} %param.14) | copy-start | bytes 6291460
  7.2 39.8 %reduce-scatter.3.cloned.1.call-start = ((), (), s32[]{:S(2)}) async-start(), calls=%async_computation.3 | async-start | bytes 2621440 | tf_op jit(solution)/shard_map/reduce_scatter | solution.py:45
  12.6 0.7 copy-start.4
  12.6 1.9 %copy-start.2 = (bf16[128,3072]{1,0:T(8,128)(2,1)S(1)}, bf16[128,3072]{1,0:T(8,128)(2,1)}, u32[]{:S(2)}) copy-start(bf16[128,3072]{1,0:T(8,128)(2,1)} %param.10) | copy-start | bytes 2359300
  12.6 19.4 %copy-start.3 = (bf16[512,128]{1,0:T(8,128)(2,1)S(1)}, bf16[512,128]{1,0:T(8,128)(2,1)}, u32[]{:S(2)}) copy-start(bf16[512,128]{1,0:T(8,128)(2,1)} %param.12) | copy-start | bytes 393220
  12.7 69.9 %all-gather.2.cloned.1.call-start = ((), (), s32[]{:S(2)}) async-start(), calls=%async_computation.2 | async-start | bytes 1310720 | tf_op jit(solution)/shard_map/all_gather | solution.py:43
  32.7 0.7 copy-start.1
  33.5 74.9 %reduce-scatter.5.cloned.1.call-start = ((), (), s32[]{:S(2)}) async-start(), calls=%async_computation.4 | async-start | bytes 1966080 | tf_op jit(solution)/shard_map/reduce_scatter | solution.py:72
Sparse Core Ops, SparseCore 0:
  12.8 34.1 reduce-scatter.2
  49.1 16.8 all-gather.1
  82.6 25.7 reduce-scatter.4
where the time goes:
time: 117 us
  blocking collectives  46.1 us (39%)
  waiting for transfers between devices  35.9 us (31%)
  between operations  14.5 us (12%)
  matrix products  13.6 us (12%)
  other arithmetic  3.54 us (3%)
  local copies, waits for them, and re-layouts  2.83 us (2%)
    psum x1, blocking collectives, body(): lax.psum(lax.cond(touches(offsets, breadth, 0, span_rows * lax.axis_size(...  30.5 us
    reduce_scatter x1, waiting for transfers between devices, body(): lax.psum_scatter(feature_parts, 'tensor', scatter_dimension=1, tiled=True)  22.4 us
    all_gather x1, blocking collectives, body(): shard_rows = lax.all_gather(reduced, 'seq', axis=0, tiled=True)  15.6 us
    reduce_scatter x1, waiting for transfers between devices, body(): lax.psum_scatter(lax.dot_general(w_up, d_up, (((1,), (1,)), ((), ())), pr...  13.4 us
    dot_general x1, matrix products, body(): lax.dot_general(w_up, d_up, (((1,), (1,)), ((), ())), preferred_element_t...  3.86 us
    dot_general x1, matrix products, body(): jnp.dot(gathered, w_up, preferred_element_type=jnp.float32)  3.45 us
    dot_general x1, matrix products, body(): lax.dot_general(d_reduced, w_in, (((1,), (1,)), ((), ())), preferred_elem...  3.22 us
    unnamed x10, local copies, waits for them, and re-layouts  2.83 us
  transfers between devices with their start and end apart: 3, of which 2 were waited for; matrix products, arithmetic and copies ran while one was open for 10% of the time, Pallas kernels for 0%

commit v1 on v0

--- a/solution.py
+++ b/solution.py
@@ -58,11 +58,14 @@
     def nothing(operand):
         return jnp.zeros((span_rows * lax.axis_size("seq"), feature_count), jnp.float32)
 
-    every_row = lax.psum(
-        lax.cond(
-            touches(offsets, breadth, 0, span_rows * lax.axis_size("seq")), compute, nothing, 0
+    every_row = jnp.sum(
+        lax.all_gather(
+            lax.cond(
+                touches(offsets, breadth, 0, span_rows * lax.axis_size("seq")), compute, nothing, 0
+            ),
+            "seq",
         ),
-        "seq",
+        axis=0,
     )
     d_reduced = lax.dynamic_slice_in_dim(every_row, lax.axis_index("seq") * span_rows, span_rows, 0)
     d_reduced = d_reduced.astype(jnp.bfloat16)

time: 117 us -> 154 us (1.32)
  waiting for transfers between devices: 35.9 us -> 101 us
  blocking collectives: 46.1 us -> 15.2 us
  other arithmetic: 3.54 us -> 5.29 us
    psum x1 -> x0, blocking collectives: 30.5 us -> none  [body(): lax.psum(lax.cond(touches(offsets, breadth, 0, span_rows * lax.axis_size(...]
    all_gather x0 -> x1, waiting for transfers between devices: none -> 29.5 us  [body(): lax.all_gather(lax.cond(touches(offsets, breadth, 0, span_rows * lax.axis...]
    reduce_scatter x1, waiting for transfers between devices: 13.4 us -> 32.4 us  [body(): lax.psum_scatter(lax.dot_general(w_up, d_up, (((1,), (1,)), ((), ())), pr...]
    all_gather x1, waiting for transfers between devices: 0.02 us -> 12.1 us  [body(): gathered = lax.all_gather(upsampled, 'tensor', axis=1, tiled=True)]
    reduce_scatter x1, waiting for transfers between devices: 22.4 us -> 27.3 us  [body(): lax.psum_scatter(feature_parts, 'tensor', scatter_dimension=1, tiled=True)]
    reduce_sum x0 -> x1, other arithmetic: none -> 1.74 us  [body(): jnp.sum(lax.all_gather(lax.cond(touches(offsets, breadth, 0, span_rows *...]
    unnamed x10 -> x12, local copies, waits for them, and re-layouts: 2.83 us -> 3.6 us
  transfers between devices with their start and end apart: 3 -> 4, of which waited for: 2 -> 4; matrix products, arithmetic and copies ran while one was open for 10% -> 7% of each run, Pallas kernels for 0% -> 0%
where the time goes in v1:
time: 154 us
  waiting for transfers between devices  101 us (66%)
  blocking collectives  15.2 us (10%)
  between operations  14.5 us (9%)
  matrix products  13.6 us (9%)
  other arithmetic  5.29 us (3%)
  local copies, waits for them, and re-layouts  3.6 us (2%)
    reduce_scatter x1, waiting for transfers between devices, body(): lax.psum_scatter(lax.dot_general(w_up, d_up, (((1,), (1,)), ((), ())), pr...  32.4 us
    all_gather x1, waiting for transfers between devices, body(): lax.all_gather(lax.cond(touches(offsets, breadth, 0, span_rows * lax.axis...  29.5 us
    reduce_scatter x1, waiting for transfers between devices, body(): lax.psum_scatter(feature_parts, 'tensor', scatter_dimension=1, tiled=True)  27.3 us
    all_gather x1, blocking collectives, body(): shard_rows = lax.all_gather(reduced, 'seq', axis=0, tiled=True)  15.2 us
    all_gather x1, waiting for transfers between devices, body(): gathered = lax.all_gather(upsampled, 'tensor', axis=1, tiled=True)  12.1 us
    dot_general x1, matrix products, body(): lax.dot_general(w_up, d_up, (((1,), (1,)), ((), ())), preferred_element_t...  3.84 us
    unnamed x12, local copies, waits for them, and re-layouts  3.6 us
    dot_general x1, matrix products, body(): jnp.dot(gathered, w_up, preferred_element_type=jnp.float32)  3.45 us
  transfers between devices with their start and end apart: 4, of which 4 were waited for; matrix products, arithmetic and copies ran while one was open for 7% of the time, Pallas kernels for 0%

profile of v1, /device:TPU:0, one launch (start us, length us, event | category | flops | bytes accessed | tf_op | source)
XLA Modules:
  0.0 153.7 jit_solution(10807686938678226894)
XLA Ops:
  7.2 1.5 copy-done
  8.8 3.8 %fusion.6 = f32[1024,512]{1,0:T(8,128)} fusion(bf16[1024,1024]{1,0:T(8,128)(2,1)S(1)} %copy-done, bf16[512,1024]{1,0:T(8,128)(2,1)} %param.15), kind=kOutput, calls=%fused_computation.16 | convolution fusion | flops 1073741824 | bytes 5242880 | tf_op jit(solution)/shard_map/dot_general | solution.py:46
  12.7 0.6 copy-done.5
  13.3 0.6 and_reduce_fusion
  14.5 32.4 %reduce-scatter.3.cloned.1.call-done = f32[256,512]{1,0:T(8,128)} async-done(((f32[1024,512]{1,0:T(8,128)}), f32[256,512]{1,0:T(8,128)}) %reduce-scatter.3.cloned.1.call-update) | async-done | bytes 524304 | tf_op jit(solution)/shard_map/reduce_scatter | solution.py:45
  46.9 1.1 convert_element_type.40
  48.0 0.8 conditional.3
  48.0 0.1 iota_subtract_fusion.1
  48.1 0.3 convolution_convert_fusion.1
  48.4 0.3 fusion.5
  48.8 0.8 copy-done.1
  49.7 1.8 %convolution_convert_fusion.3 = bf16[128,256]{1,0:T(8,128)(2,1)S(1)} fusion(bf16[128,3072]{1,0:T(8,128)(2,1)S(1)} %copy-done.3, bf16[3072,256]{1,0:T(8,128)(2,1)} %param.11), kind=kOutput, calls=%fused_computation.9 | convolution fusion | flops 201359360 | bytes 2424832 | tf_op jit(solution)/shard_map/dot_general | solution.py:25
  51.5 15.2 %all_gather.12 = bf16[512,256]{1,0:T(8,128)(2,1)S(1)} all-gather(bf16[128,256]{1,0:T(8,128)(2,1)S(1)} %convolution_convert_fusion.3), channel_id=1, replica_groups=mesh['group'=2,'seq'=4,'tensor'=4] {'seq'}, dimensions={0}, use_global_device_ids=true | all-gather | bytes 327680 | tf_op jit(solution)/shard_map/all_gather | solution.py:29
  66.7 0.7 conditional.2
  66.7 0.3 convolution_convert_fusion
  67.1 0.3 fusion.4
  67.4 0.7 copy-done.2
  68.2 29.5 %all-gather.6.cloned.1.call-done = f32[2048,256]{1,0:T(8,128)} async-done(((f32[512,256]{1,0:T(8,128)}), f32[2048,256]{1,0:T(8,128)}) %all-gather.6.cloned.1.call-update) | async-done | bytes 2097168 | tf_op jit(solution)/shard_map/all_gather | solution.py:62
  97.7 1.7 %reduce_sum.9 = bf16[512,256]{1,0:T(8,128)(2,1)S(1)} reduce(f32[4,512,256]{2,1,0:T(8,128)} %bitcast.22, f32[]{:T(128)} %constant.6.clone.1), dimensions={0}, to_apply=%region_6.0 | reduce | flops 393216 | bytes 2359300 | tf_op jit(solution)/shard_map/reduce_sum | solution.py:61
  99.4 3.2 %fusion.2 = f32[128,3072]{1,0:T(8,128)} fusion(bf16[3072,256]{1,0:T(8,128)(2,1)} %param.11, bf16[512,256]{1,0:T(8,128)(2,1)S(1)} %reduce_sum.9, s32[]{:T(128)S(6)} %select_n.3), kind=kOutput, calls=%fused_computation.11 | convolution fusion | flops 201326592 | bytes 3211268 | tf_op jit(solution)/shard_map/dot_general | solution.py:72
  102.7 12.1 %all-gather.4.cloned.1.call-done = bf16[512,1024]{1,0:T(8,128)(2,1)} async-done(((bf16[512,256]{1,0:T(8,128)(2,1)}), bf16[512,1024]{1,0:T(8,128)(2,1)}) %all-gather.4.cloned.1.call-update) | async-done | bytes 1048592 | tf_op jit(solution)/shard_map/all_gather | solution.py:43
  114.7 3.4 %convolution_convert_fusion.2 = bf16[512,1024]{1,0:T(8,128)(2,1)} fusion(bf16[512,1024]{1,0:T(8,128)(2,1)} %all-gather.4.cloned.1.call-done, bf16[1024,1024]{1,0:T(8,128)(2,1)S(1)} %copy-done), kind=kOutput, calls=%fused_computation.8 | convolution fusion | flops 1074266112 | bytes 4194304 | tf_op jit(solution)/shard_map/dot_general | solution.py:44
  118.2 27.3 %reduce-scatter.5.cloned.1.call-done = f32[128,768]{1,0:T(8,128)} async-done(((f32[128,3072]{1,0:T(8,128)}), f32[128,768]{1,0:T(8,128)}) %reduce-scatter.5.cloned.1.call-update) | async-done | bytes 393232 | tf_op jit(solution)/shard_map/reduce_scatter | solution.py:75
  145.5 1.7 %convert_element_type.42 = bf16[128,768]{1,0:T(8,128)(2,1)} convert(f32[128,768]{1,0:T(8,128)} %reduce-scatter.5.cloned.1.call-done) | non-fusion elementwise | flops 98304 | bytes 589824 | tf_op jit(solution)/shard_map/convert_element_type | solution.py:75
  (17 shorter events, 0.3 us)
Async XLA Ops:
  7.2 1.6 %copy-start = (bf16[1024,1024]{1,0:T(8,128)(2,1)S(1)}, bf16[1024,1024]{1,0:T(8,128)(2,1)}, u32[]{:S(2)}) copy-start(bf16[1024,1024]{1,0:T(8,128)(2,1)} %param.14) | copy-start | bytes 6291460
  7.2 39.7 %reduce-scatter.3.cloned.1.call-start = ((), (), s32[]{:S(2)}) async-start(), calls=%async_computation.3 | async-start | bytes 2621440 | tf_op jit(solution)/shard_map/reduce_scatter | solution.py:45
  12.6 0.7 copy-start.5
  12.6 35.4 %copy-start.4 = (bf16[512,128]{1,0:T(8,128)(2,1)S(1)}, bf16[512,128]{1,0:T(8,128)(2,1)}, u32[]{:S(2)}) copy-start(bf16[512,128]{1,0:T(8,128)(2,1)} %param.12) | copy-start | bytes 393220
  12.6 37.0 %copy-start.3 = (bf16[128,3072]{1,0:T(8,128)(2,1)S(1)}, bf16[128,3072]{1,0:T(8,128)(2,1)}, u32[]{:S(2)}) copy-start(bf16[128,3072]{1,0:T(8,128)(2,1)} %param.10) | copy-start | bytes 2359300
  12.6 85.0 %all-gather.6.cloned.1.call-start = ((), (), s32[]{:S(2)}) async-start(), calls=%async_computation.5 | async-start | bytes 2621440 | tf_op jit(solution)/shard_map/all_gather | solution.py:62
  48.8 0.8 copy-start.1
  49.6 65.1 %all-gather.4.cloned.1.call-start = ((), (), s32[]{:S(2)}) async-start(), calls=%async_computation.2 | async-start | bytes 1310720 | tf_op jit(solution)/shard_map/all_gather | solution.py:43
  67.4 0.7 copy-start.2
  68.1 77.4 %reduce-scatter.5.cloned.1.call-start = ((), (), s32[]{:S(2)}) async-start(), calls=%async_computation.4 | async-start | bytes 1966080 | tf_op jit(solution)/shard_map/reduce_scatter | solution.py:75
Sparse Core Ops, SparseCore 0:
  12.8 34.1 reduce-scatter.2
  49.7 47.9 all-gather.5
  99.3 15.3 all-gather.3
  117.3 28.1 reduce-scatter.4
